TPU v7x, 128 devices: a whole 4x4x4 slice. The times are simulated.
128 devices in a mesh: segment: 4 (over y_lo, core), slab: 32 (over z, x, y_hi).
Axes of the slice: x: 4, y: 4 (y_hi: 2, y_lo: 2; y = y_hi * 2 + y_lo), z: 4, core: 2. Of those that a mesh axis runs over, the one named last changes fastest.
Arguments:
- video_in: bfloat16 [8, 64, 64, 384], P(None, 'slab'), may hold values from -6 to 6
- cache_in: bfloat16 [4, 2, 64, 64, 384], P('segment', None, 'slab'), may hold values from -0.25 to 2
- conv_weight: bfloat16 [4, 3, 3, 3, 384, 384], P('segment'), may hold values from -0.0625 to 0.0625
- conv_bias: float32 [4, 384], P('segment'), may hold values from -1.5 to 1.5
- norm_gain: float32 [4, 384], P('segment'), may hold values from 0.5 to 2
Outputs:
- video_out: bfloat16 [8, 64, 64, 384], P('segment', 'slab')
- cache_out: bfloat16 [4, 2, 64, 64, 384], P('segment', None, 'slab')
All inputs are finite; a program needn't handle non-finite values.
Results may differ from a plain program's by a relative error of at most 0.0067.
Values may be sent and summed in bfloat16 or wider, within the bound.
A program may use at most 64 MiB of HBM per device.

v0:
```python
import jax
import jax.numpy as jnp
from jax import lax
from jax.experimental import pallas as pl
from jax.experimental.pallas import tpu as pltpu
from jax.sharding import PartitionSpec as P

MESH = pl.DeviceIdType.MESH
PITCH = 40


def kernel(video, cache, weight, bias, gain, vout, cout, wbuf, xin, cin, lhs, flat, acc, outb, actb,
           w_sem, loc_sem, in_sem, in_send, pipe_send, vin_send, cin_loc, cin_sem, cin_send, vo_send, vo_sem, co_send, co_sem):
    frames = video.shape[0]
    channels = video.shape[-1]
    rows = xin.shape[1]
    tall = rows - 2
    size = tall * PITCH
    span = rows * PITCH
    taps = weight.shape[1] // channels
    half = video.shape[2] // 2
    shift = video.shape[2] - PITCH
    lead = PITCH - half
    seg = lax.axis_index("segment")
    slab = lax.axis_index("slab")
    segs = lax.axis_size("segment")
    groups = lax.axis_size("slab") // 2
    last = segs - 1
    k = slab // 2
    hi = slab % 2
    first_seg = seg == 0
    top = k == 0
    bottom = k == groups - 1

    def at(s, kk, h):
        return (s, kk * 2 + h)

    def remote(src, dst, send, recv, dev):
        return pltpu.make_async_remote_copy(src_ref=src, dst_ref=dst, send_sem=send, recv_sem=recv, device_id=dev, device_id_type=MESH)

    def cols(h):
        return pl.ds(pl.multiple_of(h * shift, 8), PITCH)

    def own_cols(h):
        return pl.ds(pl.multiple_of(h * lead, 8), half)

    def out_cols(h):
        return pl.ds(pl.multiple_of(h * half, 8), half)

    third = weight.shape[1] // 3

    def w_copy(a, b):
        return pltpu.make_async_copy(weight.at[a, pl.ds(b * third, third), :], wbuf.at[pl.ds(b * third, third), pl.ds((2 - a) * channels, channels)], w_sem.at[a, b])

    def own_video(f):
        return pltpu.make_async_copy(video.at[f, :, cols(hi), :], xin.at[f, pl.ds(1 + 2 * hi, 2)], loc_sem.at[f])

    own_cache = pltpu.make_async_copy(cache.at[:, :, cols(hi), :], cin.at[:, pl.ds(1 + 2 * hi, 2)], cin_loc)

    own_cache.start()

    @pl.when(first_seg)
    def _():
        for f in range(frames):
            own_video(f).start()

    for a in (2, 1, 0):
        for b in range(3):
            w_copy(a, b).start()

    @pl.when(top)
    def _():
        xin[:, 0] = jnp.zeros_like(xin[:, 0])
        cin[:, 0] = jnp.zeros_like(cin[:, 0])

    @pl.when(bottom)
    def _():
        xin[:, rows - 1] = jnp.zeros_like(xin[:, rows - 1])
        cin[:, rows - 1] = jnp.zeros_like(cin[:, rows - 1])

    flat[0:8] = jnp.zeros((8, channels), jnp.float32)
    flat[8 + span:16 + span] = jnp.zeros((8, channels), jnp.float32)

    barrier = pltpu.get_barrier_semaphore()
    step_k = 2 * hi - 1
    inner = jnp.logical_and(k + step_k >= 0, k + step_k < groups)

    def greet(dev):
        pl.semaphore_signal(barrier, inc=1, device_id=dev, device_id_type=MESH)

    greet(at(seg, k, 1 - hi))
    pl.when(jnp.logical_not(top))(lambda: greet(at(seg, k - 1, 1)))
    pl.when(jnp.logical_not(bottom))(lambda: greet(at(seg, k + 1, 0)))

    @pl.when(seg > 0)
    def _():
        greet(at(seg - 1, k, hi))
        pl.when(jnp.logical_not(top))(lambda: greet(at(seg - 1, k - 1, hi)))
        pl.when(jnp.logical_not(bottom))(lambda: greet(at(seg - 1, k + 1, hi)))

    @pl.when(first_seg)
    def _():
        greet(at(2, k, 1 - hi))
        pl.when(jnp.logical_not(top))(lambda: greet(at(3 - 2 * hi, k - 1, 1)))
        pl.when(jnp.logical_not(bottom))(lambda: greet(at(1 + 2 * hi, k + 1, 0)))

    @pl.when(seg < last)
    def _():
        greet(at(last, k, 0))
        greet(at(last, k, 1))

    @pl.when(seg == last)
    def _():
        greet(at(last, k, 1 - hi))

    one = jnp.int32(1)
    zero = jnp.int32(0)
    edge_count = jnp.where(top, zero, one) + jnp.where(bottom, zero, one)
    inner_count = jnp.where(inner, one, zero)
    expected = 1 + 2 * inner_count
    expected += jnp.where(seg < last, 1 + edge_count, zero)
    expected += jnp.where(seg == 2, one, zero)
    expected += jnp.where(jnp.logical_or(seg == 1, seg == 3), inner_count, zero)
    expected += jnp.where(seg == last, 2 * last + 1, zero)
    pl.semaphore_wait(barrier, expected)

    def send_slab(f):
        return remote(video.at[f, :, cols(1 - hi), :], xin.at[f, pl.ds(1 + 2 * hi, 2)], vin_send.at[f], in_sem.at[f, 0], at(0, k, 1 - hi))

    edge_row = (rows - 1) * (1 - hi)
    edge_sem = 2 - hi

    def send_edge(f):
        to = jnp.where(seg == 1, hi, 1 - hi)
        return remote(video.at[f, hi, cols(to), :], xin.at[f, edge_row], vin_send.at[f], in_sem.at[f, edge_sem], at(0, k + step_k, to))

    def send_cache_slab():
        return remote(cache.at[:, :, cols(1 - hi), :], cin.at[:, pl.ds(1 + 2 * hi, 2)], cin_send.at[0], cin_sem.at[0], at(seg, k, 1 - hi))

    def send_cache_edge(h):
        return remote(cache.at[:, hi, cols(h), :], cin.at[:, edge_row], cin_send.at[1 + h], cin_sem.at[edge_sem], at(seg, k + step_k, h))

    @pl.when(seg == 2)
    def _():
        for f in range(frames):
            send_slab(f).start()

    @pl.when(jnp.logical_and(jnp.logical_or(seg == 1, seg == 3), inner))
    def _():
        for f in range(frames):
            send_edge(f).start()

    send_cache_slab().start()

    @pl.when(inner)
    def _():
        send_cache_edge(0).start()
        send_cache_edge(1).start()

    slot = lax.broadcasted_iota(jnp.int32, (rows, PITCH, channels), 1).reshape(span, channels)
    keep = slot != (PITCH - 1) * (1 - hi)

    def spread():
        for b in range(3):
            for c in range(3):
                start = 8 + b * PITCH + c - 1
                lhs[:, (b * 3 + c) * channels:(b * 3 + c + 1) * channels] = flat[start:start + size, :].astype(jnp.bfloat16)

    def wait_cache():
        own_cache.wait()
        remote(cache.at[:, :, cols(hi), :], cin.at[:, pl.ds(3 - 2 * hi, 2)], cin_send.at[0], cin_sem.at[0], at(seg, k, 1 - hi)).wait_recv()
        pl.when(jnp.logical_not(top))(lambda: remote(cache.at[:, 0, cols(hi), :], cin.at[:, 0], cin_send.at[1], cin_sem.at[1], at(seg, k, 1 - hi)).wait_recv())
        pl.when(jnp.logical_not(bottom))(lambda: remote(cache.at[:, 0, cols(hi), :], cin.at[:, rows - 1], cin_send.at[1], cin_sem.at[2], at(seg, k, 1 - hi)).wait_recv())

    def load_cache(j):
        values = cin[j].astype(jnp.float32).reshape(span, channels)
        flat[8:8 + span] = jnp.where(keep, values, 0.0)
        spread()

    for b in range(3):
        w_copy(0, b).wait()
        w_copy(1, b).wait()
        w_copy(2, b).wait()

    wait_cache()
    load_cache(1)
    later = jnp.dot(lhs[...], wbuf[:, channels:], preferred_element_type=jnp.float32)
    acc[0] = later[:, :channels]
    acc[1] = later[:, channels:]
    load_cache(0)
    acc[0] += jnp.dot(lhs[...], wbuf[:, 2 * channels:], preferred_element_type=jnp.float32)

    gains = gain[0:1, :]
    biases = bias[0:1, :]

    def pipe_own(f):
        return remote(outb.at[f], xin.at[f, pl.ds(1, tall)], pipe_send.at[f, 0], in_sem.at[f, 0], at(seg + 1, k, hi))

    def pipe_up(f):
        return remote(outb.at[f, 0], xin.at[f, rows - 1], pipe_send.at[f, 1], in_sem.at[f, 2], at(seg + 1, k - 1, hi))

    def pipe_down(f):
        return remote(outb.at[f, tall - 1], xin.at[f, 0], pipe_send.at[f, 2], in_sem.at[f, 1], at(seg + 1, k + 1, hi))

    per = frames // segs

    def vo_copy(f, h):
        return remote(outb.at[f, pl.ds(2 * h, 2), own_cols(hi), :], vout.at[f % per, :, out_cols(hi), :], vo_send.at[f, h], vo_sem.at[f % per, hi], at(f // per, k, h))

    def vo_local(f):
        return pltpu.make_async_copy(outb.at[f, pl.ds(2 * hi, 2), own_cols(hi), :], vout.at[f % per, :, out_cols(hi), :], vo_sem.at[f % per, hi])

    def co_copy(j):
        return remote(actb.at[j, pl.ds(2 * (1 - hi), 2), own_cols(hi), :], cout.at[j, :, out_cols(hi), :], co_send.at[j], co_sem.at[j, hi], at(seg, k, 1 - hi))

    def co_local(j):
        return pltpu.make_async_copy(actb.at[j, pl.ds(2 * hi, 2), own_cols(hi), :], cout.at[j, :, out_cols(hi), :], co_sem.at[j, hi])

    def frame(f, carry):
        @pl.when(first_seg)
        def _():
            own_video(f).wait()
            remote(video.at[f, :, cols(hi), :], xin.at[f, pl.ds(3 - 2 * hi, 2)], vin_send.at[f], in_sem.at[f, 0], at(1, k, hi)).wait_recv()

        @pl.when(seg > 0)
        def _():
            remote(outb.at[f], xin.at[f, pl.ds(1, tall)], vin_send.at[f], in_sem.at[f, 0], at(0, k, hi)).wait_recv()

        pl.when(jnp.logical_not(top))(lambda: remote(outb.at[f, 0], xin.at[f, 0], vin_send.at[f], in_sem.at[f, 1], at(0, k, 1 - hi)).wait_recv())
        pl.when(jnp.logical_not(bottom))(lambda: remote(outb.at[f, 0], xin.at[f, rows - 1], vin_send.at[f], in_sem.at[f, 2], at(0, k, 1 - hi)).wait_recv())

        values = xin[f].astype(jnp.float32).reshape(span, channels)
        mean = jnp.sum(values * values, axis=-1, keepdims=True) * (1.0 / channels)
        scaled = values * lax.rsqrt(mean + 1e-06) * gains
        acts = scaled / (1.0 + jnp.exp(-scaled))
        flat[8:8 + span] = jnp.where(keep, acts, 0.0)
        spread()

        @pl.when(f >= frames - 2)
        def _():
            j = f - (frames - 2)
            actb[j] = flat[8 + PITCH:8 + PITCH + size].reshape(tall, PITCH, channels).astype(jnp.bfloat16)
            co_copy(j).start()
            co_local(j).start()

        now = lax.rem(f, 3)
        conv = jnp.dot(lhs[...], wbuf[:, :channels], preferred_element_type=jnp.float32) + acc[now] + biases
        residual = xin[f, 1:1 + tall].astype(jnp.float32).reshape(size, channels)
        outb[f] = (residual + conv).reshape(tall, PITCH, channels).astype(jnp.bfloat16)

        @pl.when(seg < last)
        def _():
            pl.when(jnp.logical_not(top))(lambda: pipe_up(f).start())
            pl.when(jnp.logical_not(bottom))(lambda: pipe_down(f).start())
            pipe_own(f).start()

        @pl.when(seg == last)
        def _():
            @pl.when(f // per < last)
            def _():
                vo_copy(f, 0).start()
                vo_copy(f, 1).start()

            @pl.when(f // per == last)
            def _():
                vo_copy(f, 1 - hi).start()
                vo_local(f).start()

        @pl.when(f < frames - 1)
        def _():
            later = jnp.dot(lhs[...], wbuf[:, channels:], preferred_element_type=jnp.float32)
            nxt = lax.rem(f + 1, 3)
            acc[nxt] = acc[nxt] + later[:, :channels]
            acc[lax.rem(f + 2, 3)] = later[:, channels:]

        return carry

    lax.fori_loop(0, frames, frame, 0)

    for j in range(2):
        co_local(j).wait()
        co_copy(j).wait_send()
        remote(actb.at[j, pl.ds(0, 2), own_cols(hi), :], cout.at[j, :, out_cols(1 - hi), :], co_send.at[j], co_sem.at[j, 1 - hi], at(seg, k, 1 - hi)).wait_recv()

    def vo_recv(j, h):
        remote(outb.at[0, pl.ds(0, 2), own_cols(hi), :], vout.at[j, :, out_cols(h), :], vo_send.at[0, 0], vo_sem.at[j, h], at(seg, k, 1 - hi)).wait_recv()

    @pl.when(seg < last)
    def _():
        for j in range(per):
            vo_recv(j, 0)
            vo_recv(j, 1)

        def sent(f, carry):
            pipe_own(f).wait_send()
            pl.when(jnp.logical_not(top))(lambda: pipe_up(f).wait_send())
            pl.when(jnp.logical_not(bottom))(lambda: pipe_down(f).wait_send())
            return carry

        lax.fori_loop(0, frames, sent, 0)

    @pl.when(seg == last)
    def _():
        for f in range(frames):
            if f // per < last:
                vo_copy(f, 0).wait_send()
                vo_copy(f, 1).wait_send()
            else:
                vo_copy(f, 1 - hi).wait_send()
                vo_local(f).wait()
                vo_recv(f % per, 1 - hi)

    send_cache_slab().wait_send()

    @pl.when(inner)
    def _():
        send_cache_edge(0).wait_send()
        send_cache_edge(1).wait_send()

    @pl.when(seg == 2)
    def _():
        for f in range(frames):
            send_slab(f).wait_send()

    @pl.when(jnp.logical_and(jnp.logical_or(seg == 1, seg == 3), inner))
    def _():
        for f in range(frames):
            send_edge(f).wait_send()


def local(video_in, cache_in, conv_weight, conv_bias, norm_gain):
    frames, held, columns, channels = video_in.shape
    rows = 2 * held + 2
    tall = rows - 2
    size = tall * PITCH
    span = rows * PITCH
    weight = conv_weight.reshape(3, 9 * channels, channels)
    cache = cache_in[0]
    per = frames // lax.axis_size("segment")
    dma = pltpu.SemaphoreType.DMA
    video_out, cache_out = pl.pallas_call(
        kernel,
        out_shape=(
            jax.ShapeDtypeStruct((per, held, columns, channels), jnp.bfloat16),
            jax.ShapeDtypeStruct(cache.shape, jnp.bfloat16),
        ),
        in_specs=[pl.BlockSpec(memory_space=pl.ANY)] * 3 + [pl.BlockSpec(memory_space=pltpu.VMEM)] * 2,
        out_specs=(pl.BlockSpec(memory_space=pl.ANY), pl.BlockSpec(memory_space=pl.ANY)),
        scratch_shapes=[
            pltpu.VMEM((9 * channels, 3 * channels), jnp.bfloat16),
            pltpu.VMEM((frames, rows, PITCH, channels), jnp.bfloat16),
            pltpu.VMEM((2, rows, PITCH, channels), jnp.bfloat16),
            pltpu.VMEM((size, 9 * channels), jnp.bfloat16),
            pltpu.VMEM((span + 16, channels), jnp.float32),
            pltpu.VMEM((3, size, channels), jnp.float32),
            pltpu.VMEM((frames, tall, PITCH, channels), jnp.bfloat16),
            pltpu.VMEM((2, tall, PITCH, channels), jnp.bfloat16),
            dma((3, 3)), dma((frames,)), dma((frames, 3)), dma((1,)), dma((frames, 3)), dma((frames,)),
            dma, dma((3,)), dma((3,)), dma((frames, 2)), dma((per, 2)), dma((2,)), dma((2, 2)),
        ],
        compiler_params=pltpu.CompilerParams(collective_id=0, has_side_effects=True, vmem_limit_bytes=60 * 2**20),
    )(video_in, cache, weight, conv_bias, norm_gain)
    return video_out, cache_out[None]


def solution(mesh):
    return jax.shard_map(
        local,
        mesh=mesh,
        in_specs=(
            P(None, "slab", None, None),
            P("segment", None, "slab", None, None),
            P("segment", None, None, None, None, None),
            P("segment", None),
            P("segment", None),
        ),
        out_specs=(P("segment", "slab", None, None), P("segment", None, "slab", None, None)),
        check_vma=False,
    )
```

profile of v0, /device:TPU:105, one launch (start us, length us, event | category | flops | bytes accessed | tf_op | source)
XLA Modules:
  0.0 56.9 jit_solution(17564337722897836195)
XLA Ops:
  0.6 53.0 %shard_map.68 = (bf16[2,2,64,384]{3,2,1,0:T(8,128)(2,1)}, bf16[2,2,64,384]{3,2,1,0:T(8,128)(2,1)}) custom-call(bf16[8,2,64,384]{3,2,1,0:T(8,128)(2,1)} %video.1, bf16[2,2,64,384]{3,2,1,0:T(8,128)(2,1)} %bitcast.5, bf16[3,3456,384]{2,1,0:T(8,128)(2,1)} %bitcast.3, f32[1,384]{1,0:T(1,128)} %bias.1, f32[1,384]{1,0:T(1,128)} %gain.1), custom_call_target="tpu_custom_call" | custom-call | tf_op jit(solution)/shard_map/pallas_call | solution.py:341
  53.6 1.6 %copy.9 = bf16[2,2,64,384]{3,2,1,0:T(8,128)(2,1)} copy(bf16[2,2,64,384]{3,2,1,0:T(8,128)(2,1)} %get-tuple-element.8) | data formatting | bytes 393216
  55.2 1.6 %copy.10 = bf16[1,2,2,64,384]{4,3,2,1,0:T(8,128)(2,1)} copy(bf16[1,2,2,64,384]{4,3,2,1,0:T(8,128)(2,1)} %bitcast.4) | data formatting | bytes 393216
where the time goes:
time: 57.1 us; the launch traced here: 56.9 us
  Pallas kernels  53 us (93%)
  local copies, waits for them, and re-layouts  3.25 us (6%)
  between operations  0.64 us (1%)
    pallas_call x1, Pallas kernels, local(): pl.pallas_call(kernel, out_shape=(jax.ShapeDtypeStruct((per, held, column...  53 us
    unnamed x2, local copies, waits for them, and re-layouts  3.25 us

commit v1 on v0

--- a/solution.py
+++ b/solution.py
@@ -6,7 +6,7 @@
 from jax.sharding import PartitionSpec as P
 
 MESH = pl.DeviceIdType.MESH
-PITCH = 40
+PITCH = 64
 
 
 def kernel(video, cache, weight, bias, gain, vout, cout, wbuf, xin, cin, lhs, flat, acc, outb, actb,

time: 57.1 us -> 75.3 us (1.32)
  Pallas kernels: 53 us -> 71.3 us
    pallas_call x1, Pallas kernels: 53 us -> 71.3 us  [local(): pl.pallas_call(kernel, out_shape=(jax.ShapeDtypeStruct((per, held, column...]
where the time goes in v1:
time: 75.3 us; the launch traced here: 75.2 us
  Pallas kernels  71.3 us (95%)
  local copies, waits for them, and re-layouts  3.25 us (4%)
    pallas_call x1, Pallas kernels, local(): pl.pallas_call(kernel, out_shape=(jax.ShapeDtypeStruct((per, held, column...  71.3 us
    unnamed x2, local copies, waits for them, and re-layouts  3.25 us

profile of v1, /device:TPU:105, one launch (start us, length us, event | category | flops | bytes accessed | tf_op | source)
XLA Modules:
  0.0 75.2 jit_solution(1902482219118495479)
XLA Ops:
  0.6 71.3 %shard_map.68 = (bf16[2,2,64,384]{3,2,1,0:T(8,128)(2,1)}, bf16[2,2,64,384]{3,2,1,0:T(8,128)(2,1)}) custom-call(bf16[8,2,64,384]{3,2,1,0:T(8,128)(2,1)} %video.1, bf16[2,2,64,384]{3,2,1,0:T(8,128)(2,1)} %bitcast.5, bf16[3,3456,384]{2,1,0:T(8,128)(2,1)} %bitcast.3, f32[1,384]{1,0:T(1,128)} %bias.1, f32[1,384]{1,0:T(1,128)} %gain.1), custom_call_target="tpu_custom_call" | custom-call | tf_op jit(solution)/shard_map/pallas_call | solution.py:341
  71.9 1.6 %copy.9 = bf16[2,2,64,384]{3,2,1,0:T(8,128)(2,1)} copy(bf16[2,2,64,384]{3,2,1,0:T(8,128)(2,1)} %get-tuple-element.8) | data formatting | bytes 393216
  73.5 1.6 %copy.10 = bf16[1,2,2,64,384]{4,3,2,1,0:T(8,128)(2,1)} copy(bf16[1,2,2,64,384]{4,3,2,1,0:T(8,128)(2,1)} %bitcast.4) | data formatting | bytes 393216
